TPU v7x, 256 devices: a whole 4x4x8 slice. The times are simulated.
256 devices in a mesh: blk: 8 (over x, y_hi), tile: 32 (over z, y_lo, core).
Axes of the slice: x: 4, y: 4 (y_hi: 2, y_lo: 2; y = y_hi * 2 + y_lo), z: 8, core: 2. Of those that a mesh axis runs over, the one named last changes fastest.
Arguments:
- grid_feat: bfloat16 [65536, 512], P(('blk', 'tile')), may hold values from -18 to 18
- queries: bfloat16 [65536, 512], P(('blk', 'tile')), may hold values from -90 to 90
- obs_keys: bfloat16 [2048, 512], P(('blk', 'tile')), may hold values from -4 to 4
- obs_values: bfloat16 [2048, 512], P(('blk', 'tile')), may hold values from -6 to 6
- block_mask: int32 [512, 16], P(('blk', 'tile')), may hold values from 0 to 1, as said below
- obs_valid: int32 [16], replicated, may hold values from 2 to 128, as said below
- out_weight: bfloat16 [512, 512], replicated, may hold values from -0.25 to 0.25
- conv_weight: bfloat16 [3, 3, 512, 512], replicated, may hold values from -0.09375 to 0.09375
Outputs:
- layer_out: bfloat16 [65536, 512], P(('blk', 'tile'))
Inputs may be any that keep to these rules, and one draw needn't show every extreme that they name: `block_mask`: row t has a 1 in column t mod 16. `obs_valid`: at least one entry equals 128.
All inputs are finite; a program needn't handle non-finite values.
Results may differ from a plain program's by a relative error of at most 0.007.
Values may be sent and summed in bfloat16 or wider, within the bound.
A program may use at most 64 MiB of HBM per device.

v0:
```python
import jax
import jax.numpy as jnp
from jax import lax
from jax.sharding import PartitionSpec as P

HEADS = 8
OBS_BLOCK = 128


def passed_along(array, axis, by):
    peers = lax.axis_size(axis)
    return lax.ppermute(array, axis, [(i, (i + by) % peers) for i in range(peers)])


def with_halo(block, sides, width):
    for axis, dim in sides:
        count = lax.axis_size(axis)
        forward = [(i, i + 1) for i in range(count - 1)]
        backward = [(target, source) for source, target in forward]
        low = lax.ppermute(
            lax.slice_in_dim(block, block.shape[dim] - width, None, axis=dim), axis, forward
        )
        high = lax.ppermute(lax.slice_in_dim(block, 0, width, axis=dim), axis, backward)
        block = jnp.concatenate([low, block, high], axis=dim)
    return block


def circulate(block, visit, carry):
    home = lax.axis_index("blk")
    count = lax.axis_size("blk")
    carry = visit(carry, block, home)
    for step in range(1, count):
        block = passed_along(block, "blk", 1)
        carry = visit(carry, block, (home - step) % count)
    return carry


def on_device(
    grid_feat, queries, obs_keys, obs_values, block_mask, obs_valid, out_weight, conv_weight
):
    q_dev, width = queries.shape
    head = width // HEADS
    scale = head ** (-0.5)
    tiles = block_mask.shape[0]
    nblocks = block_mask.shape[1]
    lon = q_dev // tiles
    group_rows = obs_keys.shape[0] * lax.axis_size("tile")
    query_heads = queries.reshape(q_dev, HEADS, head)
    mask_float = block_mask.astype(jnp.float32)
    block_ids = jnp.arange(nblocks, dtype=jnp.int32)

    def attend(carry, kv_rows, start):
        rows = kv_rows.shape[1]
        key_index = start + jnp.arange(rows, dtype=jnp.int32)
        member = (key_index // OBS_BLOCK)[:, None] == block_ids[None, :]
        limits = jnp.sum(jnp.where(member, obs_valid[None, :], 0), axis=1)
        live = key_index % OBS_BLOCK < limits
        wanted = (
            jnp.dot(mask_float, member.astype(jnp.float32).T, precision=lax.Precision.HIGHEST) > 0.5
        )
        allowed = wanted & live[None, :]
        top, total, acc = carry
        keys = kv_rows[0].reshape(rows, HEADS, head)
        values = kv_rows[1].reshape(rows, HEADS, head)
        scores = (
            jnp.einsum("qhd,khd->hqk", query_heads, keys, preferred_element_type=jnp.float32)
            * scale
        )
        scores = scores.reshape(HEADS, tiles, lon, rows)
        scores = jnp.where(allowed[None, :, None, :], scores, -jnp.inf).reshape(HEADS, q_dev, rows)
        new_top = jnp.maximum(top, jnp.max(scores, axis=-1))
        factor = jnp.exp(top - new_top)
        weights = jnp.exp(scores - new_top[..., None])
        total = total * factor + jnp.sum(weights, axis=-1)
        acc = acc * factor[..., None] + jnp.einsum(
            "hqk,khd->hqd", weights.astype(jnp.bfloat16), values, preferred_element_type=jnp.float32
        )
        return (new_top, total, acc)

    start_state = (
        jnp.full((HEADS, q_dev), -1e30, jnp.float32),
        jnp.zeros((HEADS, q_dev), jnp.float32),
        jnp.zeros((HEADS, q_dev, head), jnp.float32),
    )
    kv_local = jnp.stack([obs_keys, obs_values])

    def visit_shards(carry, block, owner):
        collected = lax.all_gather(block, "tile", axis=1, tiled=True)
        return attend(carry, collected, owner * group_rows)

    state = circulate(kv_local, visit_shards, start_state)
    top, total, acc = state
    mixed = (
        jnp.transpose(acc / total[..., None], (1, 0, 2)).reshape(q_dev, width).astype(jnp.bfloat16)
    )
    projected = jnp.dot(mixed, out_weight, preferred_element_type=jnp.float32)
    hidden = lax.optimization_barrier(
        (grid_feat.astype(jnp.float32) + projected).astype(jnp.bfloat16)
    )
    wide = hidden.astype(jnp.float32)
    normed = (wide * lax.rsqrt(jnp.mean(wide * wide, axis=-1, keepdims=True) + 1e-06)).astype(
        jnp.bfloat16
    )
    field = normed.reshape(tiles, lon, width)
    padded = with_halo(field, ((("blk", "tile"), 0),), 1)
    summed = jnp.zeros((q_dev, width), jnp.float32)
    for lat_off in range(3):
        for lon_off in range(3):
            moved = jnp.roll(padded[lat_off : lat_off + tiles], 1 - lon_off, axis=1)
            summed = summed + jnp.dot(
                moved.reshape(q_dev, width),
                conv_weight[lat_off, lon_off],
                preferred_element_type=jnp.float32,
            )
    return (wide + summed).astype(jnp.bfloat16)


def solution(mesh):
    in_specs = (
        P(("blk", "tile"), None),
        P(("blk", "tile"), None),
        P(("blk", "tile"), None),
        P(("blk", "tile"), None),
        P(("blk", "tile"), None),
        P(),
        P(),
        P(),
    )
    out_specs = P(("blk", "tile"), None)
    return jax.shard_map(
        on_device, mesh=mesh, in_specs=in_specs, out_specs=out_specs, check_vma=False
    )
```

profile of v0, /device:TPU:1, one launch (start us, length us, event | category | flops | bytes accessed | tf_op | source)
XLA Modules:
  0.0 375.5 jit_solution(6822890569749922319)
XLA Ops:
  0.0 1.4 pad_maximum_fusion.6
  1.4 3.7 collective-permute-start
  5.1 38.9 %all_gather.24 = bf16[2,256,512]{2,1,0:T(8,128)(2,1)S(1)} all-gather(bf16[2,8,512]{2,1,0:T(8,128)(2,1)} %pad_maximum_fusion.6), channel_id=1, replica_groups=mesh['blk'=8,'tile'=32] {'tile'}, dimensions={1}, use_global_device_ids=true | all-gather | bytes 540672 | tf_op jit(solution)/shard_map/all_gather | solution.py:88
  44.2 1.1 copy.84
  46.0 0.8 fusion.51
  46.8 0.8 fusion.49
  48.5 0.8 fusion.45
  49.3 1.4 fusion.43
  50.7 1.3 fusion.41
  59.5 0.8 copy.85
  60.4 32.3 %all_gather.25 = bf16[2,256,512]{2,1,0:T(8,128)(2,1)S(1)} all-gather(bf16[2,8,512]{2,1,0:T(8,128)(2,1)} %collective-permute-done), channel_id=1, replica_groups=mesh['blk'=8,'tile'=32] {'tile'}, dimensions={1}, use_global_device_ids=true | all-gather | bytes 540672 | tf_op jit(solution)/shard_map/all_gather | solution.py:88
  92.8 0.9 copy.88
  93.6 2.4 collective-permute-start.1
  96.0 2.8 fusion.161
  98.8 0.8 copy.89
  100.6 34.7 %all_gather.26 = bf16[2,256,512]{2,1,0:T(8,128)(2,1)S(1)} all-gather(bf16[2,8,512]{2,1,0:T(8,128)(2,1)S(1)} %collective-permute-done.1), channel_id=1, replica_groups=mesh['blk'=8,'tile'=32] {'tile'}, dimensions={1}, use_global_device_ids=true | all-gather | bytes 540672 | tf_op jit(solution)/shard_map/all_gather | solution.py:88
  135.4 0.8 copy.92
  137.0 3.4 fusion.160
  140.3 0.8 copy.93
  141.2 1.4 collective-permute-done.2
  143.2 33.1 %all_gather.27 = bf16[2,256,512]{2,1,0:T(8,128)(2,1)S(1)} all-gather(bf16[2,8,512]{2,1,0:T(8,128)(2,1)S(1)} %collective-permute-done.2), channel_id=1, replica_groups=mesh['blk'=8,'tile'=32] {'tile'}, dimensions={1}, use_global_device_ids=true | all-gather | bytes 540672 | tf_op jit(solution)/shard_map/all_gather | solution.py:88
  176.4 0.8 copy.96
  177.5 3.4 fusion.159
  180.9 0.9 copy.97
  181.8 1.9 collective-permute-done.3
  184.2 34.7 %all_gather.28 = bf16[2,256,512]{2,1,0:T(8,128)(2,1)S(1)} all-gather(bf16[2,8,512]{2,1,0:T(8,128)(2,1)S(1)} %collective-permute-done.3), channel_id=1, replica_groups=mesh['blk'=8,'tile'=32] {'tile'}, dimensions={1}, use_global_device_ids=true | all-gather | bytes 540672 | tf_op jit(solution)/shard_map/all_gather | solution.py:88
  219.0 0.8 copy.100
  219.8 2.9 fusion.158
  223.3 0.8 copy.101
  224.2 4.7 %collective-permute-done.4 = bf16[2,8,512]{2,1,0:T(8,128)(2,1)S(1)} collective-permute-done((bf16[2,8,512]{2,1,0:T(8,128)(2,1)S(1)}, bf16[2,8,512]{2,1,0:T(8,128)(2,1)S(1)}, u32[]{:S(2)}, u32[]{:S(2)}) %collective-permute-start.4) | collective-permute-done | bytes 16416 | tf_op jit(solution)/shard_map/ppermute | solution.py:12
  229.5 33.1 %all_gather.29 = bf16[2,256,512]{2,1,0:T(8,128)(2,1)S(1)} all-gather(bf16[2,8,512]{2,1,0:T(8,128)(2,1)S(1)} %collective-permute-done.4), channel_id=1, replica_groups=mesh['blk'=8,'tile'=32] {'tile'}, dimensions={1}, use_global_device_ids=true | all-gather | bytes 540672 | tf_op jit(solution)/shard_map/all_gather | solution.py:88
  262.7 0.9 copy.104
  263.5 3.5 fusion.157
  267.0 0.8 copy.105
  267.8 2.1 collective-permute-done.5
  270.5 34.7 %all_gather.30 = bf16[2,256,512]{2,1,0:T(8,128)(2,1)S(1)} all-gather(bf16[2,8,512]{2,1,0:T(8,128)(2,1)S(1)} %collective-permute-done.5), channel_id=1, replica_groups=mesh['blk'=8,'tile'=32] {'tile'}, dimensions={1}, use_global_device_ids=true | all-gather | bytes 540672 | tf_op jit(solution)/shard_map/all_gather | solution.py:88
  305.3 0.8 copy.108
  306.1 3.4 fusion.156
  309.5 0.8 copy.109
  310.3 2.2 collective-permute-done.6
  312.5 33.1 %all_gather.31 = bf16[2,256,512]{2,1,0:T(8,128)(2,1)S(1)} all-gather(bf16[2,8,512]{2,1,0:T(8,128)(2,1)S(1)} %collective-permute-done.6), channel_id=1, replica_groups=mesh['blk'=8,'tile'=32] {'tile'}, dimensions={1}, use_global_device_ids=true | all-gather | bytes 540672 | tf_op jit(solution)/shard_map/all_gather | solution.py:88
  345.7 0.8 copy.112
  346.7 1.6 fusion.155
  349.7 1.0 copy-done.2
  361.7 3.5 collective-permute-start.7
  365.2 1.9 collective-permute-start.8
  367.2 4.3 %collective-permute-done.8 = bf16[1,128,512]{2,1,0:T(8,128)(2,1)S(1)} collective-permute-done((bf16[1,128,512]{2,1,0:T(8,128)(2,1)S(1)}, bf16[1,128,512]{2,1,0:T(8,128)(2,1)S(1)}, u32[]{:S(2)}, u32[]{:S(2)}) %collective-permute-start.8) | collective-permute-done | bytes 131104 | tf_op jit(solution)/shard_map/ppermute | solution.py:23
  374.5 1.0 fusion.33
  (152 shorter events, 29.8 us)
Async XLA Ops:
  0.0 360.4 %copy-start = (bf16[512,512]{1,0:T(8,128)(2,1)S(1)}, bf16[512,512]{1,0:T(8,128)(2,1)}, u32[]{:S(2)}) copy-start(bf16[512,512]{1,0:T(8,128)(2,1)} %param.14) | copy-start | bytes 1572868
  1.4 59.0 %collective-permute-start = (bf16[2,8,512]{2,1,0:T(8,128)(2,1)}, bf16[2,8,512]{2,1,0:T(8,128)(2,1)}, u32[]{:S(2)}, u32[]{:S(2)}) collective-permute-start(bf16[2,8,512]{2,1,0:T(8,128)(2,1)} %pad_maximum_fusion.6), channel_id=1, source_target_pairs={{0,32},{32,64},{64,96},{96,128},{128,160},{160,192},{192,224},{224... | collective-permute-start | bytes 49160 | tf_op jit(solution)/shard_map/ppermute | solution.py:12
  53.1 0.7 copy-start.29
  93.6 6.4 %collective-permute-start.1 = (bf16[2,8,512]{2,1,0:T(8,128)(2,1)}, bf16[2,8,512]{2,1,0:T(8,128)(2,1)S(1)}, u32[]{:S(2)}, u32[]{:S(2)}) collective-permute-start(bf16[2,8,512]{2,1,0:T(8,128)(2,1)} %collective-permute-done), channel_id=1, source_target_pairs={{0,32},{32,64},{64,96},{96,128},{128,160},{160,192},{192,224},{224... | collective-permute-start | bytes 49160 | tf_op jit(solution)/shard_map/ppermute | solution.py:12
  100.1 0.6 copy-start.25
  136.2 6.4 %collective-permute-start.2 = (bf16[2,8,512]{2,1,0:T(8,128)(2,1)}, bf16[2,8,512]{2,1,0:T(8,128)(2,1)S(1)}, u32[]{:S(2)}, u32[]{:S(2)}) collective-permute-start(bf16[2,8,512]{2,1,0:T(8,128)(2,1)} %copy-done.25), channel_id=1, source_target_pairs={{0,32},{32,64},{64,96},{96,128},{128,160},{160,192},{192,224},{224... | collective-permute-start | bytes 49160 | tf_op jit(solution)/shard_map/ppermute | solution.py:12
  142.6 0.6 copy-start.26
  177.2 6.4 %collective-permute-start.3 = (bf16[2,8,512]{2,1,0:T(8,128)(2,1)}, bf16[2,8,512]{2,1,0:T(8,128)(2,1)S(1)}, u32[]{:S(2)}, u32[]{:S(2)}) collective-permute-start(bf16[2,8,512]{2,1,0:T(8,128)(2,1)} %copy-done.26), channel_id=1, source_target_pairs={{0,32},{32,64},{64,96},{96,128},{128,160},{160,192},{192,224},{224... | collective-permute-start | bytes 49160 | tf_op jit(solution)/shard_map/ppermute | solution.py:12
  183.6 0.6 copy-start.23
  219.8 2.9 copy-start.24
  219.8 2.9 copy-start.15
  219.8 2.9 copy-start.17
  222.7 6.2 %copy-start.19 = (f32[8,256]{1,0:T(8,128)}, f32[8,256]{1,0:T(8,128)S(1)}, u32[]{:S(2)}) copy-start(f32[8,256]{1,0:T(8,128)S(1)} %get-tuple-element.75) | copy-start | bytes 24580
  222.7 6.2 %collective-permute-start.4 = (bf16[2,8,512]{2,1,0:T(8,128)(2,1)S(1)}, bf16[2,8,512]{2,1,0:T(8,128)(2,1)S(1)}, u32[]{:S(2)}, u32[]{:S(2)}) collective-permute-start(bf16[2,8,512]{2,1,0:T(8,128)(2,1)S(1)} %copy-done.24), channel_id=1, source_target_pairs={{0,32},{32,64},{64,96},{96,128},{128,160},{160,192},{192,224},{224... | collective-permute-start | bytes 49160 | tf_op jit(solution)/shard_map/ppermute | solution.py:12
  228.9 0.6 copy-start.28
  263.5 6.4 %collective-permute-start.5 = (bf16[2,8,512]{2,1,0:T(8,128)(2,1)}, bf16[2,8,512]{2,1,0:T(8,128)(2,1)S(1)}, u32[]{:S(2)}, u32[]{:S(2)}) collective-permute-start(bf16[2,8,512]{2,1,0:T(8,128)(2,1)} %copy-done.28), channel_id=1, source_target_pairs={{0,32},{32,64},{64,96},{96,128},{128,160},{160,192},{192,224},{224... | collective-permute-start | bytes 49160 | tf_op jit(solution)/shard_map/ppermute | solution.py:12
  269.9 0.6 copy-start.27
  306.1 6.4 %collective-permute-start.6 = (bf16[2,8,512]{2,1,0:T(8,128)(2,1)}, bf16[2,8,512]{2,1,0:T(8,128)(2,1)S(1)}, u32[]{:S(2)}, u32[]{:S(2)}) collective-permute-start(bf16[2,8,512]{2,1,0:T(8,128)(2,1)} %copy-done.27), channel_id=1, source_target_pairs={{0,32},{32,64},{64,96},{96,128},{128,160},{160,192},{192,224},{224... | collective-permute-start | bytes 49160 | tf_op jit(solution)/shard_map/ppermute | solution.py:12
  345.7 2.6 copy-start.16
  346.7 2.7 copy-start.1
  349.1 1.6 copy-start.2
  349.4 2.0 copy-start.3
  350.7 1.7 copy-start.4
  351.4 1.7 copy-start.5
  352.4 1.7 copy-start.6
  354.2 0.7 copy-start.18
  354.2 0.7 copy-start.20
  354.2 0.7 copy-start.21
  354.2 0.7 copy-start.22
  354.2 1.0 copy-start.7
  354.5 1.2 copy-start.8
  355.7 1.0 copy-start.9
  356.1 1.0 copy-start.10
  357.1 1.0 copy-start.11
  357.6 1.0 copy-start.12
  358.5 1.0 copy-start.13
  359.5 12.6 %slice-start = ((s8[4718592]{0:T(1024)(128)(4,1)}), s8[4194304]{0:T(1024)(128)(4,1)S(1)}, s32[]{:S(2)}) async-start(s8[4718592]{0:T(1024)(128)(4,1)} %bitcast.311), calls=%async_computation | async-start | bytes 8388608
  359.9 1.2 copy-start.14
  361.1 10.9 %slice-start.1 = ((s8[4718592]{0:T(1024)(128)(4,1)}), s8[524288]{0:T(1024)(128)(4,1)S(1)}, s32[]{:S(2)}) async-start(s8[4718592]{0:T(1024)(128)(4,1)} %bitcast.311), calls=%async_computation.1 | async-start | bytes 1048576
  361.7 5.4 %collective-permute-start.7 = (bf16[1,128,512]{2,1,0:T(8,128)(2,1)S(1)}, bf16[1,128,512]{2,1,0:T(8,128)(2,1)S(1)}, u32[]{:S(2)}, u32[]{:S(2)}) collective-permute-start(bf16[1,128,512]{2,1,0:T(8,128)(2,1)S(1)} %get-tuple-element.63), channel_id=1, source_target_pairs={{0,1},{1,2},{2,3},{3,4},{4,5},{5,6},{6,7},{7,8},{8,9},{9,10},{10,1... | collective-permute-start | bytes 393224 | tf_op jit(solution)/shard_map/ppermute | solution.py:20
  365.2 6.3 %collective-permute-start.8 = (bf16[1,128,512]{2,1,0:T(8,128)(2,1)S(1)}, bf16[1,128,512]{2,1,0:T(8,128)(2,1)S(1)}, u32[]{:S(2)}, u32[]{:S(2)}) collective-permute-start(bf16[1,128,512]{2,1,0:T(8,128)(2,1)S(1)} %get-tuple-element.62), channel_id=1, source_target_pairs={{1,0},{2,1},{3,2},{4,3},{5,4},{6,5},{7,6},{8,7},{9,8},{10,9},{11,1... | collective-permute-start | bytes 393224 | tf_op jit(solution)/shard_map/ppermute | solution.py:23
where the time goes:
time: 376 us
  blocking collectives  275 us (73%)
  matrix products  35.6 us (9%)
  local copies, waits for them, and re-layouts  28 us (7%)
  waiting for transfers between devices  17.1 us (5%)
  starting transfers between devices  12.6 us (3%)
  other arithmetic  6.82 us (2%)
    all_gather x8, blocking collectives, visit_shards(): collected = lax.all_gather(block, 'tile', axis=1, tiled=True)  275 us
    dot_general x8, matrix products, attend(): jnp.einsum('qhd,khd->hqk', query_heads, keys, preferred_element_type=jnp....  21.3 us
    ppermute x7, waiting for transfers between devices, passed_along(): lax.ppermute(array, axis, [(i, (i + by) % peers) for i in range(peers)])  12.8 us
    unnamed x65, local copies, waits for them, and re-layouts  9.9 us
  transfers between devices with their start and end apart: 9, of which 7 were waited for; matrix products, arithmetic and copies ran while one was open for 10% of the time, Pallas kernels for 0%

commit v1 on v0

--- a/solution.py
+++ b/solution.py
@@ -85,7 +85,9 @@
     kv_local = jnp.stack([obs_keys, obs_values])
 
     def visit_shards(carry, block, owner):
-        collected = lax.all_gather(block, "tile", axis=1, tiled=True)
+        collected = jnp.concatenate(
+            lax.all_to_all(jnp.stack([block] * lax.axis_size("tile")), "tile", 0, 0), axis=1
+        )
         return attend(carry, collected, owner * group_rows)
 
     state = circulate(kv_local, visit_shards, start_state)

time: 376 us -> 231 us (0.61)
  blocking collectives: 275 us -> 0 us
  starting transfers between devices: 12.6 us -> 70.7 us
  waiting for transfers between devices: 17.1 us -> 74.7 us
  local copies, waits for them, and re-layouts: 28 us -> 49.6 us
  matrix products: 35.6 us -> 27.9 us
    all_gather x8 -> x0, blocking collectives: 275 us -> none  [visit_shards(): collected = lax.all_gather(block, 'tile', axis=1, tiled=True)]
    all_to_all x0 -> x8, waiting for transfers between devices: none -> 56 us  [visit_shards(): lax.all_to_all(jnp.stack([block] * lax.axis_size('tile')), 'tile', 0, 0)]
    all_to_all x0 -> x8, starting transfers between devices: none -> 49 us  [visit_shards(): lax.all_to_all(jnp.stack([block] * lax.axis_size('tile')), 'tile', 0, 0)]
    another operation x0 -> x24, local copies, waits for them, and re-layouts: none -> 29.3 us  [the longest x8 13.7 us: attend(): keys = kv_rows[0].reshape(rows, HEADS, head)]
    ppermute x7, starting transfers between devices: 7.17 us -> 15.6 us  [passed_along(): lax.ppermute(array, axis, [(i, (i + by) % peers) for i in range(peers)])]
    slice x9 -> x0, local copies, waits for them, and re-layouts: 6.07 us -> none  [attend(): keys = kv_rows[0].reshape(rows, HEADS, head)]
    dot_general x8, matrix products: 6.87 us -> 1.02 us  [attend(): jnp.dot(mask_float, member.astype(jnp.float32).T, precision=lax.Precision...]
    unnamed x65 -> x51, local copies, waits for them, and re-layouts: 9.9 us -> 6.46 us
  transfers between devices with their start and end apart: 9 -> 17, of which waited for: 7 -> 13; matrix products, arithmetic and copies ran while one was open for 10% -> 23% of each run, Pallas kernels for 0% -> 0%
where the time goes in v1:
time: 231 us; the launch traced here: 228 us
  waiting for transfers between devices  74.7 us (32%)
  starting transfers between devices  70.7 us (31%)
  local copies, waits for them, and re-layouts  49.6 us (21%)
  matrix products  27.9 us (12%)
  other arithmetic  4.26 us (2%)
    all_to_all x8, waiting for transfers between devices, visit_shards(): lax.all_to_all(jnp.stack([block] * lax.axis_size('tile')), 'tile', 0, 0)  56 us
    all_to_all x8, starting transfers between devices, visit_shards(): lax.all_to_all(jnp.stack([block] * lax.axis_size('tile')), 'tile', 0, 0)  49 us
    dot_general x8, matrix products, attend(): jnp.einsum('qhd,khd->hqk', query_heads, keys, preferred_element_type=jnp....  19.6 us
    ppermute x7, starting transfers between devices, passed_along(): lax.ppermute(array, axis, [(i, (i + by) % peers) for i in range(peers)])  15.6 us
    ppermute x7, waiting for transfers between devices, passed_along(): lax.ppermute(array, axis, [(i, (i + by) % peers) for i in range(peers)])  14.4 us
    another operation x8, local copies, waits for them, and re-layouts, attend(): keys = kv_rows[0].reshape(rows, HEADS, head)  13.7 us
    slice x8, local copies, waits for them, and re-layouts, attend(): values = kv_rows[1].reshape(rows, HEADS, head)  8.64 us
    another operation x8, local copies, waits for them, and re-layouts, attend(): values = kv_rows[1].reshape(rows, HEADS, head)  7.82 us
  transfers between devices with their start and end apart: 17, of which 13 were waited for; matrix products, arithmetic and copies ran while one was open for 23% of the time, Pallas kernels for 0%

profile of v1, /device:TPU:1, one launch (start us, length us, event | category | flops | bytes accessed | tf_op | source)
XLA Modules:
  0.0 227.9 jit_solution(18233171363771840418)
XLA Ops:
  1.6 11.3 %all-to-all-start = ((bf16[32,2,8,512]{3,2,1,0:T(8,128)(2,1)}), bf16[32,2,8,512]{3,2,1,0:T(8,128)(2,1)S(1)}, u32[]{:S(2)}, u32[]{:S(2)}) async-start(bf16[32,2,8,512]{3,2,1,0:T(8,128)(2,1)} %stack.25), calls=%async_computation | async-start | bytes 1048576 | tf_op jit(solution)/shard_map/all_to_all | solution.py:89
  12.9 2.7 %collective-permute-start = (bf16[2,8,512]{2,1,0:T(8,128)(2,1)S(1)}, bf16[2,8,512]{2,1,0:T(8,128)(2,1)S(1)}, u32[]{:S(2)}, u32[]{:S(2)}) collective-permute-start(bf16[2,8,512]{2,1,0:T(8,128)(2,1)S(1)} %pad_maximum_fusion.6), channel_id=1, source_target_pairs={{0,32},{32,64},{64,96},{96,128},{128,160},{160,192},{192,224},{224... | collective-permute-start | bytes 49160 | tf_op jit(solution)/shard_map/ppermute | solution.py:12
  15.6 3.6 %collective-permute-done = bf16[2,8,512]{2,1,0:T(8,128)(2,1)S(1)} collective-permute-done((bf16[2,8,512]{2,1,0:T(8,128)(2,1)S(1)}, bf16[2,8,512]{2,1,0:T(8,128)(2,1)S(1)}, u32[]{:S(2)}, u32[]{:S(2)}) %collective-permute-start) | collective-permute-done | bytes 16416 | tf_op jit(solution)/shard_map/ppermute | solution.py:12
  19.3 10.4 %all-to-all-done = bf16[32,2,8,512]{3,2,1,0:T(8,128)(2,1)S(1)} async-done(((bf16[32,2,8,512]{3,2,1,0:T(8,128)(2,1)}), bf16[32,2,8,512]{3,2,1,0:T(8,128)(2,1)S(1)}, u32[]{:S(2)}, u32[]{:S(2)}) %all-to-all-start) | async-done | bytes 524320 | tf_op jit(solution)/shard_map/all_to_all | solution.py:89
  30.5 5.1 %all-to-all-start.1 = ((bf16[32,2,8,512]{3,2,1,0:T(8,128)(2,1)}), bf16[32,2,8,512]{3,2,1,0:T(8,128)(2,1)S(1)}, u32[]{:S(2)}, u32[]{:S(2)}) async-start(bf16[32,2,8,512]{3,2,1,0:T(8,128)(2,1)} %stack.26), calls=%async_computation.1 | async-start | bytes 1048576 | tf_op jit(solution)/shard_map/all_to_all | solution.py:89
  35.8 2.7 %collective-permute-start.1 = (bf16[2,8,512]{2,1,0:T(8,128)(2,1)S(1)}, bf16[2,8,512]{2,1,0:T(8,128)(2,1)S(1)}, u32[]{:S(2)}, u32[]{:S(2)}) collective-permute-start(bf16[2,8,512]{2,1,0:T(8,128)(2,1)S(1)} %collective-permute-done), channel_id=1, source_target_pairs={{0,32},{32,64},{64,96},{96,128},{128,160},{160,192},{192,224},{224... | collective-permute-start | bytes 49160 | tf_op jit(solution)/shard_map/ppermute | solution.py:12
  38.6 3.6 %collective-permute-done.1 = bf16[2,8,512]{2,1,0:T(8,128)(2,1)S(1)} collective-permute-done((bf16[2,8,512]{2,1,0:T(8,128)(2,1)S(1)}, bf16[2,8,512]{2,1,0:T(8,128)(2,1)S(1)}, u32[]{:S(2)}, u32[]{:S(2)}) %collective-permute-start.1) | collective-permute-done | bytes 16416 | tf_op jit(solution)/shard_map/ppermute | solution.py:12
  42.3 10.4 %all-to-all-done.1 = bf16[32,2,8,512]{3,2,1,0:T(8,128)(2,1)S(1)} async-done(((bf16[32,2,8,512]{3,2,1,0:T(8,128)(2,1)}), bf16[32,2,8,512]{3,2,1,0:T(8,128)(2,1)S(1)}, u32[]{:S(2)}, u32[]{:S(2)}) %all-to-all-start.1) | async-done | bytes 524320 | tf_op jit(solution)/shard_map/all_to_all | solution.py:89
  53.5 5.0 %all-to-all-start.2 = ((bf16[32,2,8,512]{3,2,1,0:T(8,128)(2,1)}), bf16[32,2,8,512]{3,2,1,0:T(8,128)(2,1)S(1)}, u32[]{:S(2)}, u32[]{:S(2)}) async-start(bf16[32,2,8,512]{3,2,1,0:T(8,128)(2,1)} %stack.27), calls=%async_computation.2 | async-start | bytes 1048576 | tf_op jit(solution)/shard_map/all_to_all | solution.py:89
  58.8 2.7 %collective-permute-start.2 = (bf16[2,8,512]{2,1,0:T(8,128)(2,1)S(1)}, bf16[2,8,512]{2,1,0:T(8,128)(2,1)S(1)}, u32[]{:S(2)}, u32[]{:S(2)}) collective-permute-start(bf16[2,8,512]{2,1,0:T(8,128)(2,1)S(1)} %collective-permute-done.1), channel_id=1, source_target_pairs={{0,32},{32,64},{64,96},{96,128},{128,160},{160,192},{192,224},{224... | collective-permute-start | bytes 49160 | tf_op jit(solution)/shard_map/ppermute | solution.py:12
  61.6 3.6 %collective-permute-done.2 = bf16[2,8,512]{2,1,0:T(8,128)(2,1)S(1)} collective-permute-done((bf16[2,8,512]{2,1,0:T(8,128)(2,1)S(1)}, bf16[2,8,512]{2,1,0:T(8,128)(2,1)S(1)}, u32[]{:S(2)}, u32[]{:S(2)}) %collective-permute-start.2) | collective-permute-done | bytes 16416 | tf_op jit(solution)/shard_map/ppermute | solution.py:12
  65.2 10.4 %all-to-all-done.2 = bf16[32,2,8,512]{3,2,1,0:T(8,128)(2,1)S(1)} async-done(((bf16[32,2,8,512]{3,2,1,0:T(8,128)(2,1)}), bf16[32,2,8,512]{3,2,1,0:T(8,128)(2,1)S(1)}, u32[]{:S(2)}, u32[]{:S(2)}) %all-to-all-start.2) | async-done | bytes 524320 | tf_op jit(solution)/shard_map/all_to_all | solution.py:89
  76.5 4.8 %all-to-all-start.3 = ((bf16[32,2,8,512]{3,2,1,0:T(8,128)(2,1)}), bf16[32,2,8,512]{3,2,1,0:T(8,128)(2,1)S(1)}, u32[]{:S(2)}, u32[]{:S(2)}) async-start(bf16[32,2,8,512]{3,2,1,0:T(8,128)(2,1)} %stack.28), calls=%async_computation.3 | async-start | bytes 1048576 | tf_op jit(solution)/shard_map/all_to_all | solution.py:89
  81.7 2.7 %collective-permute-start.3 = (bf16[2,8,512]{2,1,0:T(8,128)(2,1)S(1)}, bf16[2,8,512]{2,1,0:T(8,128)(2,1)S(1)}, u32[]{:S(2)}, u32[]{:S(2)}) collective-permute-start(bf16[2,8,512]{2,1,0:T(8,128)(2,1)S(1)} %collective-permute-done.2), channel_id=1, source_target_pairs={{0,32},{32,64},{64,96},{96,128},{128,160},{160,192},{192,224},{224... | collective-permute-start | bytes 49160 | tf_op jit(solution)/shard_map/ppermute | solution.py:12
  84.4 3.6 %collective-permute-done.3 = bf16[2,8,512]{2,1,0:T(8,128)(2,1)S(1)} collective-permute-done((bf16[2,8,512]{2,1,0:T(8,128)(2,1)S(1)}, bf16[2,8,512]{2,1,0:T(8,128)(2,1)S(1)}, u32[]{:S(2)}, u32[]{:S(2)}) %collective-permute-start.3) | collective-permute-done | bytes 16416 | tf_op jit(solution)/shard_map/ppermute | solution.py:12
  88.8 9.6 %all-to-all-done.3 = bf16[32,2,8,512]{3,2,1,0:T(8,128)(2,1)S(1)} async-done(((bf16[32,2,8,512]{3,2,1,0:T(8,128)(2,1)}), bf16[32,2,8,512]{3,2,1,0:T(8,128)(2,1)S(1)}, u32[]{:S(2)}, u32[]{:S(2)}) %all-to-all-start.3) | async-done | bytes 524320 | tf_op jit(solution)/shard_map/all_to_all | solution.py:89
  99.3 5.5 %all-to-all-start.4 = ((bf16[32,2,8,512]{3,2,1,0:T(8,128)(2,1)}), bf16[32,2,8,512]{3,2,1,0:T(8,128)(2,1)}, u32[]{:S(2)}, u32[]{:S(2)}) async-start(bf16[32,2,8,512]{3,2,1,0:T(8,128)(2,1)} %stack.29), calls=%async_computation.4 | async-start | bytes 1048576 | tf_op jit(solution)/shard_map/all_to_all | solution.py:89
  105.0 2.7 %collective-permute-start.5 = (bf16[2,8,512]{2,1,0:T(8,128)(2,1)S(1)}, bf16[2,8,512]{2,1,0:T(8,128)(2,1)S(1)}, u32[]{:S(2)}, u32[]{:S(2)}) collective-permute-start(bf16[2,8,512]{2,1,0:T(8,128)(2,1)S(1)} %collective-permute-done.4), channel_id=1, source_target_pairs={{0,32},{32,64},{64,96},{96,128},{128,160},{160,192},{192,224},{224... | collective-permute-start | bytes 49160 | tf_op jit(solution)/shard_map/ppermute | solution.py:12
  113.1 1.4 collective-permute-start.6
  115.9 1.8 fusion.178
  119.1 2.9 %all-to-all-done.4 = bf16[32,2,8,512]{3,2,1,0:T(8,128)(2,1)} async-done(((bf16[32,2,8,512]{3,2,1,0:T(8,128)(2,1)}), bf16[32,2,8,512]{3,2,1,0:T(8,128)(2,1)}, u32[]{:S(2)}, u32[]{:S(2)}) %all-to-all-start.4) | async-done | bytes 524320 | tf_op jit(solution)/shard_map/all_to_all | solution.py:89
  122.9 6.2 %all-to-all-start.5 = ((bf16[32,2,8,512]{3,2,1,0:T(8,128)(2,1)}), bf16[32,2,8,512]{3,2,1,0:T(8,128)(2,1)}, u32[]{:S(2)}, u32[]{:S(2)}) async-start(bf16[32,2,8,512]{3,2,1,0:T(8,128)(2,1)} %stack.30), calls=%async_computation.5 | async-start | bytes 1048576 | tf_op jit(solution)/shard_map/all_to_all | solution.py:89
  129.0 1.6 fusion.177
  131.4 2.0 reshape_squeeze.52
  134.5 2.9 %fusion.176 = (f32[8,256]{1,0:T(8,128)S(1)}, f32[8,256,256]{1,2,0:T(8,128)}) fusion(bf16[256,8,64]{0,2,1:T(8,128)(2,1)} %bitcast.360, bf16[256,8,64]{2,1,0:T(8,128)(2,1)} %reshape_squeeze.52, pred[256,256]{0,1:T(8,128)(4,1)} %copy.116), kind=kOutput, calls=%fused_computation.326 | convolution fusion | flops 68679680 | bytes 2695168 | tf_op jit(solution)/shard_map/qhd,khd->hqk/dot_general | solution.py:66
  138.2 2.1 reshape_squeeze.54
  141.3 4.5 %all-to-all-done.5 = bf16[32,2,8,512]{3,2,1,0:T(8,128)(2,1)} async-done(((bf16[32,2,8,512]{3,2,1,0:T(8,128)(2,1)}), bf16[32,2,8,512]{3,2,1,0:T(8,128)(2,1)}, u32[]{:S(2)}, u32[]{:S(2)}) %all-to-all-start.5) | async-done | bytes 524320 | tf_op jit(solution)/shard_map/all_to_all | solution.py:89
  146.7 5.7 %all-to-all-start.6 = ((bf16[32,2,8,512]{3,2,1,0:T(8,128)(2,1)}), bf16[32,2,8,512]{3,2,1,0:T(8,128)(2,1)}, u32[]{:S(2)}, u32[]{:S(2)}) async-start(bf16[32,2,8,512]{3,2,1,0:T(8,128)(2,1)} %stack.31), calls=%async_computation.6 | async-start | bytes 1048576 | tf_op jit(solution)/shard_map/all_to_all | solution.py:89
  152.4 2.9 %fusion.175 = (f32[8,256]{1,0:T(8,128)S(1)}, f32[8,256,256]{1,2,0:T(8,128)}) fusion(bf16[256,8,64]{0,2,1:T(8,128)(2,1)} %bitcast.361, bf16[256,8,64]{2,1,0:T(8,128)(2,1)} %reshape_squeeze.54, pred[256,256]{0,1:T(8,128)(4,1)} %copy.120), kind=kOutput, calls=%fused_computation.325 | convolution fusion | flops 68679680 | bytes 2695168 | tf_op jit(solution)/shard_map/qhd,khd->hqk/dot_general | solution.py:66
  155.3 1.8 fusion.165
  157.1 2.0 reshape_squeeze.56
  159.1 2.9 %fusion.174 = (f32[8,256]{1,0:T(8,128)S(1)}, f32[8,256,256]{1,2,0:T(8,128)}) fusion(bf16[256,8,64]{0,2,1:T(8,128)(2,1)} %bitcast.362, bf16[256,8,64]{2,1,0:T(8,128)(2,1)} %reshape_squeeze.56, pred[256,256]{0,1:T(8,128)(4,1)} %copy.124), kind=kOutput, calls=%fused_computation.324 | convolution fusion | flops 68679680 | bytes 2695168 | tf_op jit(solution)/shard_map/qhd,khd->hqk/dot_general | solution.py:66
  163.1 6.4 %all-to-all-done.6 = bf16[32,2,8,512]{3,2,1,0:T(8,128)(2,1)} async-done(((bf16[32,2,8,512]{3,2,1,0:T(8,128)(2,1)}), bf16[32,2,8,512]{3,2,1,0:T(8,128)(2,1)}, u32[]{:S(2)}, u32[]{:S(2)}) %all-to-all-start.6) | async-done | bytes 524320 | tf_op jit(solution)/shard_map/all_to_all | solution.py:89
  169.6 1.6 stack.32
  171.1 5.5 %all-to-all-start.7 = ((bf16[32,2,8,512]{3,2,1,0:T(8,128)(2,1)}), bf16[32,2,8,512]{3,2,1,0:T(8,128)(2,1)}, u32[]{:S(2)}, u32[]{:S(2)}) async-start(bf16[32,2,8,512]{3,2,1,0:T(8,128)(2,1)} %stack.32), calls=%async_computation.7 | async-start | bytes 1048576 | tf_op jit(solution)/shard_map/all_to_all | solution.py:89
  176.6 1.8 fusion.164
  178.4 2.1 reshape_squeeze.58
  181.6 2.9 %fusion.173 = (f32[8,256]{1,0:T(8,128)S(1)}, f32[8,256,256]{1,2,0:T(8,128)}) fusion(bf16[256,8,64]{0,2,1:T(8,128)(2,1)} %bitcast.363, bf16[256,8,64]{2,1,0:T(8,128)(2,1)} %reshape_squeeze.58, pred[256,256]{0,1:T(8,128)(4,1)} %copy.128), kind=kOutput, calls=%fused_computation.323 | convolution fusion | flops 68679680 | bytes 2695168 | tf_op jit(solution)/shard_map/qhd,khd->hqk/dot_general | solution.py:66
  184.5 1.8 fusion.163
  186.3 2.1 reshape_squeeze.60
  189.4 2.9 %fusion.172 = (f32[8,256]{1,0:T(8,128)S(1)}, f32[8,256,256]{1,2,0:T(8,128)}) fusion(bf16[256,8,64]{0,2,1:T(8,128)(2,1)} %bitcast.364, bf16[256,8,64]{2,1,0:T(8,128)(2,1)} %reshape_squeeze.60, pred[256,256]{0,1:T(8,128)(4,1)} %copy.132), kind=kOutput, calls=%fused_computation.322 | convolution fusion | flops 68679680 | bytes 2695168 | tf_op jit(solution)/shard_map/qhd,khd->hqk/dot_general | solution.py:66
  192.3 1.4 all-to-all-done.7
  193.8 1.8 fusion.162
  195.5 2.1 reshape_squeeze.62
  198.7 1.7 fusion.171
  213.4 4.3 %collective-permute-start.7 = (bf16[1,128,512]{2,1,0:T(8,128)(2,1)S(1)}, bf16[1,128,512]{2,1,0:T(8,128)(2,1)S(1)}, u32[]{:S(2)}, u32[]{:S(2)}) collective-permute-start(bf16[1,128,512]{2,1,0:T(8,128)(2,1)S(1)} %get-tuple-element.63), channel_id=1, source_target_pairs={{0,1},{1,2},{2,3},{3,4},{4,5},{5,6},{6,7},{7,8},{8,9},{9,10},{10,1... | collective-permute-start | bytes 393224 | tf_op jit(solution)/shard_map/ppermute | solution.py:20
  217.6 1.9 collective-permute-start.8
  219.6 4.3 %collective-permute-done.8 = bf16[1,128,512]{2,1,0:T(8,128)(2,1)S(1)} collective-permute-done((bf16[1,128,512]{2,1,0:T(8,128)(2,1)S(1)}, bf16[1,128,512]{2,1,0:T(8,128)(2,1)S(1)}, u32[]{:S(2)}, u32[]{:S(2)}) %collective-permute-start.8) | collective-permute-done | bytes 131104 | tf_op jit(solution)/shard_map/ppermute | solution.py:23
  (154 shorter events, 41.8 us)
Async XLA Ops:
  0.0 212.1 %copy-start = (bf16[512,512]{1,0:T(8,128)(2,1)S(1)}, bf16[512,512]{1,0:T(8,128)(2,1)}, u32[]{:S(2)}) copy-start(bf16[512,512]{1,0:T(8,128)(2,1)} %param.14) | copy-start | bytes 1572868
  0.0 38.5 %copy-start.21 = (s32[16]{0:T(128)S(1)}, s32[16]{0:T(128)}, u32[]{:S(2)}) copy-start(s32[16]{0:T(128)} %param.13) | copy-start | bytes 196
  1.6 56.9 %copy-start.22 = (s32[2,16]{1,0:T(2,128)S(1)}, s32[2,16]{1,0:T(2,128)}, u32[]{:S(2)}) copy-start(s32[2,16]{1,0:T(2,128)} %param.12) | copy-start | bytes 388
  1.6 28.0 %all-to-all-start = ((bf16[32,2,8,512]{3,2,1,0:T(8,128)(2,1)}), bf16[32,2,8,512]{3,2,1,0:T(8,128)(2,1)S(1)}, u32[]{:S(2)}, u32[]{:S(2)}) async-start(bf16[32,2,8,512]{3,2,1,0:T(8,128)(2,1)} %stack.25), calls=%async_computation | async-start | bytes 1048576 | tf_op jit(solution)/shard_map/all_to_all | solution.py:89
  12.9 6.3 %collective-permute-start = (bf16[2,8,512]{2,1,0:T(8,128)(2,1)S(1)}, bf16[2,8,512]{2,1,0:T(8,128)(2,1)S(1)}, u32[]{:S(2)}, u32[]{:S(2)}) collective-permute-start(bf16[2,8,512]{2,1,0:T(8,128)(2,1)S(1)} %pad_maximum_fusion.6), channel_id=1, source_target_pairs={{0,32},{32,64},{64,96},{96,128},{128,160},{160,192},{192,224},{224... | collective-permute-start | bytes 49160 | tf_op jit(solution)/shard_map/ppermute | solution.py:12
  30.5 22.2 %all-to-all-start.1 = ((bf16[32,2,8,512]{3,2,1,0:T(8,128)(2,1)}), bf16[32,2,8,512]{3,2,1,0:T(8,128)(2,1)S(1)}, u32[]{:S(2)}, u32[]{:S(2)}) async-start(bf16[32,2,8,512]{3,2,1,0:T(8,128)(2,1)} %stack.26), calls=%async_computation.1 | async-start | bytes 1048576 | tf_op jit(solution)/shard_map/all_to_all | solution.py:89
  35.8 6.4 %collective-permute-start.1 = (bf16[2,8,512]{2,1,0:T(8,128)(2,1)S(1)}, bf16[2,8,512]{2,1,0:T(8,128)(2,1)S(1)}, u32[]{:S(2)}, u32[]{:S(2)}) collective-permute-start(bf16[2,8,512]{2,1,0:T(8,128)(2,1)S(1)} %collective-permute-done), channel_id=1, source_target_pairs={{0,32},{32,64},{64,96},{96,128},{128,160},{160,192},{192,224},{224... | collective-permute-start | bytes 49160 | tf_op jit(solution)/shard_map/ppermute | solution.py:12
  53.5 54.5 %copy-start.19 = (bf16[256,512]{1,0:T(8,128)(2,1)S(1)}, bf16[256,512]{1,0:T(8,128)(2,1)}, u32[]{:S(2)}) copy-start(bf16[256,512]{1,0:T(8,128)(2,1)} %param.9) | copy-start | bytes 786436
  53.5 22.0 %all-to-all-start.2 = ((bf16[32,2,8,512]{3,2,1,0:T(8,128)(2,1)}), bf16[32,2,8,512]{3,2,1,0:T(8,128)(2,1)S(1)}, u32[]{:S(2)}, u32[]{:S(2)}) async-start(bf16[32,2,8,512]{3,2,1,0:T(8,128)(2,1)} %stack.27), calls=%async_computation.2 | async-start | bytes 1048576 | tf_op jit(solution)/shard_map/all_to_all | solution.py:89
  58.8 6.4 %collective-permute-start.2 = (bf16[2,8,512]{2,1,0:T(8,128)(2,1)S(1)}, bf16[2,8,512]{2,1,0:T(8,128)(2,1)S(1)}, u32[]{:S(2)}, u32[]{:S(2)}) collective-permute-start(bf16[2,8,512]{2,1,0:T(8,128)(2,1)S(1)} %collective-permute-done.1), channel_id=1, source_target_pairs={{0,32},{32,64},{64,96},{96,128},{128,160},{160,192},{192,224},{224... | collective-permute-start | bytes 49160 | tf_op jit(solution)/shard_map/ppermute | solution.py:12
  75.6 33.4 %copy-start.12 = (bf16[32,2,8,512]{3,2,1,0:T(8,128)(2,1)}, bf16[32,2,8,512]{3,2,1,0:T(8,128)(2,1)S(1)}, u32[]{:S(2)}) copy-start(bf16[32,2,8,512]{3,2,1,0:T(8,128)(2,1)S(1)} %all-to-all-done.2) | copy-start | bytes 1572868
  76.5 21.9 %all-to-all-start.3 = ((bf16[32,2,8,512]{3,2,1,0:T(8,128)(2,1)}), bf16[32,2,8,512]{3,2,1,0:T(8,128)(2,1)S(1)}, u32[]{:S(2)}, u32[]{:S(2)}) async-start(bf16[32,2,8,512]{3,2,1,0:T(8,128)(2,1)} %stack.28), calls=%async_computation.3 | async-start | bytes 1048576 | tf_op jit(solution)/shard_map/all_to_all | solution.py:89
  81.7 6.3 %collective-permute-start.3 = (bf16[2,8,512]{2,1,0:T(8,128)(2,1)S(1)}, bf16[2,8,512]{2,1,0:T(8,128)(2,1)S(1)}, u32[]{:S(2)}, u32[]{:S(2)}) collective-permute-start(bf16[2,8,512]{2,1,0:T(8,128)(2,1)S(1)} %collective-permute-done.2), channel_id=1, source_target_pairs={{0,32},{32,64},{64,96},{96,128},{128,160},{160,192},{192,224},{224... | collective-permute-start | bytes 49160 | tf_op jit(solution)/shard_map/ppermute | solution.py:12
  88.0 17.0 %collective-permute-start.4 = (bf16[2,8,512]{2,1,0:T(8,128)(2,1)S(1)}, bf16[2,8,512]{2,1,0:T(8,128)(2,1)S(1)}, u32[]{:S(2)}, u32[]{:S(2)}) collective-permute-start(bf16[2,8,512]{2,1,0:T(8,128)(2,1)S(1)} %collective-permute-done.3), channel_id=1, source_target_pairs={{0,32},{32,64},{64,96},{96,128},{128,160},{160,192},{192,224},{224... | collective-permute-start | bytes 49160 | tf_op jit(solution)/shard_map/ppermute | solution.py:12
  98.4 16.1 %copy-start.14 = (bf16[32,2,8,512]{3,2,1,0:T(8,128)(2,1)}, bf16[32,2,8,512]{3,2,1,0:T(8,128)(2,1)S(1)}, u32[]{:S(2)}) copy-start(bf16[32,2,8,512]{3,2,1,0:T(8,128)(2,1)S(1)} %all-to-all-done.3) | copy-start | bytes 1572868
  99.3 22.6 %all-to-all-start.4 = ((bf16[32,2,8,512]{3,2,1,0:T(8,128)(2,1)}), bf16[32,2,8,512]{3,2,1,0:T(8,128)(2,1)}, u32[]{:S(2)}, u32[]{:S(2)}) async-start(bf16[32,2,8,512]{3,2,1,0:T(8,128)(2,1)} %stack.29), calls=%async_computation.4 | async-start | bytes 1048576 | tf_op jit(solution)/shard_map/all_to_all | solution.py:89
  105.0 8.1 %collective-permute-start.5 = (bf16[2,8,512]{2,1,0:T(8,128)(2,1)S(1)}, bf16[2,8,512]{2,1,0:T(8,128)(2,1)S(1)}, u32[]{:S(2)}, u32[]{:S(2)}) collective-permute-start(bf16[2,8,512]{2,1,0:T(8,128)(2,1)S(1)} %collective-permute-done.4), channel_id=1, source_target_pairs={{0,32},{32,64},{64,96},{96,128},{128,160},{160,192},{192,224},{224... | collective-permute-start | bytes 49160 | tf_op jit(solution)/shard_map/ppermute | solution.py:12
  108.1 20.9 %copy-start.20 = (bf16[256,512]{0,1:T(8,128)(2,1)}, bf16[256,512]{0,1:T(8,128)(2,1)S(1)}, u32[]{:S(2)}) copy-start(bf16[256,512]{0,1:T(8,128)(2,1)S(1)} %copy.108) | copy-start | bytes 786436
  113.1 50.0 %collective-permute-start.6 = (bf16[2,8,512]{2,1,0:T(8,128)(2,1)S(1)}, bf16[2,8,512]{2,1,0:T(8,128)(2,1)}, u32[]{:S(2)}, u32[]{:S(2)}) collective-permute-start(bf16[2,8,512]{2,1,0:T(8,128)(2,1)S(1)} %collective-permute-done.5), channel_id=1, source_target_pairs={{0,32},{32,64},{64,96},{96,128},{128,160},{160,192},{192,224},{224... | collective-permute-start | bytes 49160 | tf_op jit(solution)/shard_map/ppermute | solution.py:12
  122.9 23.0 %all-to-all-start.5 = ((bf16[32,2,8,512]{3,2,1,0:T(8,128)(2,1)}), bf16[32,2,8,512]{3,2,1,0:T(8,128)(2,1)}, u32[]{:S(2)}, u32[]{:S(2)}) async-start(bf16[32,2,8,512]{3,2,1,0:T(8,128)(2,1)} %stack.30), calls=%async_computation.5 | async-start | bytes 1048576 | tf_op jit(solution)/shard_map/all_to_all | solution.py:89
  129.0 1.6 copy-start.13
  134.5 2.9 %copy-start.15 = (bf16[32,2,8,512]{3,2,1,0:T(8,128)(2,1)S(1)}, bf16[32,2,8,512]{3,2,1,0:T(8,128)(2,1)}, u32[]{:S(2)}) copy-start(bf16[32,2,8,512]{3,2,1,0:T(8,128)(2,1)} %copy-done.14) | copy-start | bytes 1572868
  146.7 22.8 %all-to-all-start.6 = ((bf16[32,2,8,512]{3,2,1,0:T(8,128)(2,1)}), bf16[32,2,8,512]{3,2,1,0:T(8,128)(2,1)}, u32[]{:S(2)}, u32[]{:S(2)}) async-start(bf16[32,2,8,512]{3,2,1,0:T(8,128)(2,1)} %stack.31), calls=%async_computation.6 | async-start | bytes 1048576 | tf_op jit(solution)/shard_map/all_to_all | solution.py:89
  171.1 22.6 %all-to-all-start.7 = ((bf16[32,2,8,512]{3,2,1,0:T(8,128)(2,1)}), bf16[32,2,8,512]{3,2,1,0:T(8,128)(2,1)}, u32[]{:S(2)}, u32[]{:S(2)}) async-start(bf16[32,2,8,512]{3,2,1,0:T(8,128)(2,1)} %stack.32), calls=%async_computation.7 | async-start | bytes 1048576 | tf_op jit(solution)/shard_map/all_to_all | solution.py:89
  198.7 1.8 copy-start.6
  200.5 1.6 copy-start.1
  200.8 2.0 copy-start.2
  202.1 1.7 copy-start.3
  202.8 1.7 copy-start.4
  203.8 1.7 copy-start.5
  205.6 1.0 copy-start.16
  207.1 1.0 copy-start.7
  207.5 1.1 copy-start.8
  208.5 1.1 copy-start.9
  209.0 1.1 copy-start.10
  210.0 1.1 copy-start.11
  210.6 1.1 copy-start.17
  211.1 13.3 %slice-start = ((s8[4718592]{0:T(1024)(128)(4,1)}), s8[4194304]{0:T(1024)(128)(4,1)S(1)}, s32[]{:S(2)}) async-start(s8[4718592]{0:T(1024)(128)(4,1)} %bitcast.343), calls=%async_computation.8 | async-start | bytes 8388608
  211.6 1.2 copy-start.18
  212.8 11.7 %slice-start.1 = ((s8[4718592]{0:T(1024)(128)(4,1)}), s8[524288]{0:T(1024)(128)(4,1)S(1)}, s32[]{:S(2)}) async-start(s8[4718592]{0:T(1024)(128)(4,1)} %bitcast.343), calls=%async_computation.9 | async-start | bytes 1048576
  213.4 6.2 %collective-permute-start.7 = (bf16[1,128,512]{2,1,0:T(8,128)(2,1)S(1)}, bf16[1,128,512]{2,1,0:T(8,128)(2,1)S(1)}, u32[]{:S(2)}, u32[]{:S(2)}) collective-permute-start(bf16[1,128,512]{2,1,0:T(8,128)(2,1)S(1)} %get-tuple-element.63), channel_id=1, source_target_pairs={{0,1},{1,2},{2,3},{3,4},{4,5},{5,6},{6,7},{7,8},{8,9},{9,10},{10,1... | collective-permute-start | bytes 393224 | tf_op jit(solution)/shard_map/ppermute | solution.py:20
  217.6 6.3 %collective-permute-start.8 = (bf16[1,128,512]{2,1,0:T(8,128)(2,1)S(1)}, bf16[1,128,512]{2,1,0:T(8,128)(2,1)S(1)}, u32[]{:S(2)}, u32[]{:S(2)}) collective-permute-start(bf16[1,128,512]{2,1,0:T(8,128)(2,1)S(1)} %get-tuple-element.62), channel_id=1, source_target_pairs={{1,0},{2,1},{3,2},{4,3},{5,4},{6,5},{7,6},{8,7},{9,8},{10,9},{11,1... | collective-permute-start | bytes 393224 | tf_op jit(solution)/shard_map/ppermute | solution.py:23
